TPU v7x, 32 devices: a whole 2x2x4 slice. The times are simulated.
32 devices in a mesh: group: 2 (over x), blk: 16 (over z, y, core).
Axes of the slice: x: 2, y: 2, z: 4, core: 2. Of those that a mesh axis runs over, the one named last changes fastest.
Arguments:
- spectra: bfloat16 [2, 2048, 768], P(None, ('group', 'blk')), parts along dimension 1, may hold values from -6 to 6
- gap_mask: int32 [2048, 48], P(('group', 'blk')), parts along dimension 0, may hold values 0 or 1
Outputs:
- correlation: float32 [8, 2048, 1024], P(None, ('group', 'blk')), parts along dimension 1
There are 2 independent parts, one for each index of `group`. A program takes and returns all parts, laid end to end along the dimension named above; each array names one. Nothing has to cross between parts.
All inputs are finite; a program needn't handle non-finite values. No bound on the sum of `gap_mask` on one device may be relied on, other than what follows from the above.
Results may differ from a plain program's by a relative error of at most 0.0085.
Values may be sent and summed in bfloat16 or wider, within the bound.
A program may use at most 192 MiB of HBM per device.

v0:
```python
import math

import jax
import jax.numpy as jnp
from jax import lax
from jax.sharding import PartitionSpec as P

LAGS = 8


level_floor = 0.3
first_bin = 96.0


def from_behind(array, axis, by):
    size = lax.axis_size(axis)
    return lax.ppermute(array, axis, [(i, (i + by) % size) for i in range(size)])


def band_table(bin_count):
    ladder = jnp.arange(bin_count, dtype=jnp.int32)
    near = (jnp.abs(ladder[:, None] - ladder[None, :]) <= 2).astype(jnp.float32)
    return near / jnp.sum(near, axis=0, keepdims=True)


def phase_tables(bin_count, lag_count):
    freq = first_bin + jnp.arange(bin_count, dtype=jnp.float32)
    shifts = 3.0 + 5.0 * jnp.arange(lag_count, dtype=jnp.float32)
    theta = 2.0 * math.pi * freq[:, None] * shifts[None, :] / 512.0
    return (jnp.cos(theta), jnp.sin(theta))


def whiten(spectra, gap_mask):
    members = spectra.shape[1]
    win_count = gap_mask.shape[1]
    bin_count = spectra.shape[2] // win_count
    parts = spectra.astype(jnp.float32).reshape(2, members, win_count, bin_count)
    amplitude = jnp.sqrt(parts[0] * parts[0] + parts[1] * parts[1])
    level = jnp.einsum(
        "swg,gf->swf", amplitude, band_table(bin_count), precision=lax.Precision.HIGHEST
    )
    level = jnp.maximum(level, level_floor)
    factor = gap_mask.astype(jnp.float32)[None, :, :, None] / level[None]
    return (parts * factor).astype(jnp.bfloat16)


def modulate(whitened, lag_count):
    members = whitened.shape[1]
    win_count = whitened.shape[2]
    bin_count = whitened.shape[3]
    cosine, sine = phase_tables(bin_count, lag_count)
    scale = 1.0 / math.sqrt(win_count * bin_count)
    values = whitened.astype(jnp.float32)
    cos_rows = cosine.T[:, None, None, None, :]
    sin_rows = sine.T[:, None, None, None, :]
    even_mod = (cos_rows * values[None] * scale).astype(jnp.bfloat16)
    swapped = jnp.stack([values[1], -values[0]])
    odd_mod = (sin_rows * swapped[None] * scale).astype(jnp.bfloat16)
    stacked = jnp.stack([even_mod, odd_mod])
    stacked = jnp.transpose(stacked, (0, 1, 3, 2, 4, 5))
    return stacked.reshape(2 * lag_count * members, 2 * win_count * bin_count)


def per_device(spectra, gap_mask):
    cycle_size = lax.axis_size("blk")
    position = lax.axis_index("blk")
    members = spectra.shape[1]
    whitened = whiten(spectra, gap_mask)
    modulated = modulate(whitened, LAGS)
    own_block = jnp.transpose(whitened, (1, 0, 2, 3)).reshape(members, -1)
    zero = jnp.int32(0)

    def correlate(other):
        sums = jnp.einsum("ak,tk->at", modulated, other, preferred_element_type=jnp.float32)
        return sums.reshape(2, LAGS, members, members)

    def deposit(tiles, product, offset):
        slot = (position + offset) % cycle_size
        return lax.dynamic_update_slice(tiles, product[None], (slot, zero, zero, zero))

    tiles = jnp.zeros((cycle_size, LAGS, members, members), jnp.float32)
    own_sums = correlate(own_block)
    tiles = deposit(tiles, own_sums[0] - own_sums[1], 0)

    def step_ahead(moving):
        return from_behind(moving, "blk", -1)

    def advance_two(offset, carried):
        forward_block, behind, tiles = carried
        forward_block = step_ahead(forward_block)
        behind = from_behind(behind, "blk", 1)
        sums = correlate(forward_block)
        tiles = deposit(tiles, sums[0] - sums[1], offset)
        back_sums = correlate(behind)
        tiles = deposit(tiles, back_sums[0] - back_sums[1], cycle_size - offset)
        return (forward_block, behind, tiles)

    forward_block, behind, tiles = lax.fori_loop(
        1, cycle_size // 2, advance_two, (own_block, own_block, tiles)
    )
    forward_block = step_ahead(forward_block)
    last_sums = correlate(forward_block)
    tiles = deposit(tiles, last_sums[0] - last_sums[1], cycle_size // 2)
    return jnp.transpose(tiles, (1, 2, 0, 3)).reshape(LAGS, members, cycle_size * members)


def solution(mesh):
    placed = (P(None, ("group", "blk"), None), P(("group", "blk"), None))
    return jax.shard_map(
        per_device,
        mesh=mesh,
        in_specs=placed,
        out_specs=P(None, ("group", "blk"), None),
        check_vma=False,
    )
```

profile of v0, /device:TPU:0, one launch (start us, length us, event | category | flops | bytes accessed | tf_op | source)
XLA Modules:
  0.0 170.6 jit_solution(18170119916723445467)
XLA Ops:
  3.1 1.8 %multiply_convert_fusion = (bf16[1,8,2,64,48,16]{3,1,0,5,4,2:T(8,128)(2,1)S(1)}, bf16[1,8,2,64,48,16]{3,1,0,5,4,2:T(8,128)(2,1)S(1)}) fusion(f32[2,64,48,16]{1,3,2,0:T(8,128)S(1)} %pad_maximum_fusion, f32[8,16]{0,1:T(8,128)S(1)} %get-tuple-element.184, f32[2,64,48,16]{1,3,2,0:T(8,128)S(1)} %get-tuple-element.181, f32[8,16]{0,1:T(8,128)S(1)} %get-tuple-element.183), kind=kLoop, calls=%fused_computation.5 | loop fusion | flops 4718592 | bytes 3933184 | tf_op jit(solution)/shard_map/convert_element_type | solution.py:58
  4.9 4.1 %maximum_bitcast_fusion = bf16[2,8,64,2,48,16]{2,1,0,5,4,3:T(8,128)(2,1)} fusion(bf16[1,8,2,64,48,16]{3,1,0,5,4,2:T(8,128)(2,1)S(1)} %get-tuple-element.185, bf16[1,8,2,64,48,16]{3,1,0,5,4,2:T(8,128)(2,1)S(1)} %get-tuple-element.186), kind=kLoop, calls=%fused_computation.4 | loop fusion | flops 1572864 | bytes 6291456 | tf_op jit(solution)/shard_map/transpose | solution.py:60
  9.0 9.4 %reshape.233 = bf16[1024,1536]{0,1:T(8,128)(2,1)} reshape(bf16[2,8,64,2,48,16]{2,1,0,5,4,3:T(8,128)(2,1)} %maximum_bitcast_fusion) | data formatting | bytes 6291456 | tf_op jit(solution)/shard_map/reshape | solution.py:61
  18.4 3.2 %copy.10 = bf16[1024,1536]{1,0:T(8,128)(2,1)S(1)} copy(bf16[1024,1536]{0,1:T(8,128)(2,1)} %reshape.233) | data formatting | bytes 6291456 | tf_op jit(solution)/shard_map/while | solution.py:98
  21.6 3.3 %fusion.13 = f32[1024,64]{0,1:T(8,128)} fusion(bf16[1024,1536]{0,1:T(8,128)(2,1)} %reshape.233, bf16[64,1536]{0,1:T(8,128)(2,1)S(1)} %bitcast.44), kind=kOutput, calls=%fused_computation.35 | convolution fusion | flops 201326592 | bytes 3604480 | tf_op jit(solution)/shard_map/ak,tk->at/dot_general | solution.py:74
  28.9 1.9 %copy-done.1 = f32[16,8,64,64]{2,1,3,0:T(8,128)} copy-done((f32[16,8,64,64]{2,1,3,0:T(8,128)}, f32[16,8,64,64]{2,1,3,0:T(8,128)S(1)}, u32[]{:S(2)}) %copy-start.1) | copy-done | bytes 2097176
  30.8 128.0 %while.19 = (s32[]{:T(128)}, bf16[64,1536]{1,0:T(8,128)(2,1)}, bf16[64,1536]{1,0:T(8,128)(2,1)}, f32[16,8,64,64]{2,1,3,0:T(8,128)}, bf16[1024,1536]{1,0:T(8,128)...) while((s32[]{:T(128)}, bf16[64,1536]{1,0:T(8,128)(2,1)}, ...), condition=%wide.region_2.3_spmd, body=%wide.region_1.2_spmd.sunk | while | flops 402718720 | bytes 12583451 | solution.py:98
  30.8 5.5 %collective-permute-start = (bf16[64,1536]{1,0:T(8,128)(2,1)}, bf16[64,1536]{1,0:T(8,128)(2,1)S(1)}, u32[]{:S(2)}, u32[]{:S(2)}) collective-permute-start(bf16[64,1536]{1,0:T(8,128)(2,1)} %get-tuple-element.235), channel_id=1, source_target_pairs={{0,15},{1,0},{2,1},{3,2},{4,3},{5,4},{6,5},{7,6},{8,7},{9,8},{10,9... | collective-permute-start | bytes 589832 | tf_op jit(solution)/shard_map/while/body/eval_jaxpr/ppermute | solution.py:17
  36.3 3.5 %collective-permute-done = bf16[64,1536]{1,0:T(8,128)(2,1)S(1)} collective-permute-done((bf16[64,1536]{1,0:T(8,128)(2,1)}, bf16[64,1536]{1,0:T(8,128)(2,1)S(1)}, u32[]{:S(2)}, u32[]{:S(2)}) %collective-permute-start) | collective-permute-done | bytes 196640 | tf_op jit(solution)/shard_map/while/body/eval_jaxpr/ppermute | solution.py:17
  41.0 3.4 %collective-permute-done.1 = bf16[64,1536]{1,0:T(8,128)(2,1)} collective-permute-done((bf16[64,1536]{1,0:T(8,128)(2,1)}, bf16[64,1536]{1,0:T(8,128)(2,1)}, u32[]{:S(2)}, u32[]{:S(2)}) %collective-permute-start.1) | collective-permute-done | bytes 196640 | tf_op jit(solution)/shard_map/while/body/eval_jaxpr/ppermute | solution.py:17
  44.4 2.0 %fusion.35 = f32[1024,64]{0,1:T(8,128)S(1)} fusion(bf16[1024,1536]{1,0:T(8,128)(2,1)S(1)} %get-tuple-element.248, bf16[64,1536]{1,0:T(8,128)(2,1)} %collective-permute-done.1), kind=kOutput, calls=%fused_computation.34.clone.1 | convolution fusion | flops 201326592 | bytes 3604480 | tf_op jit(solution)/shard_map/while/body/eval_jaxpr/ak,tk->at/dot_general | solution.py:74
  54.0 3.5 %collective-permute-done = bf16[64,1536]{1,0:T(8,128)(2,1)S(1)} collective-permute-done((bf16[64,1536]{1,0:T(8,128)(2,1)}, bf16[64,1536]{1,0:T(8,128)(2,1)S(1)}, u32[]{:S(2)}, u32[]{:S(2)}) %collective-permute-start) | collective-permute-done | bytes 196640 | tf_op jit(solution)/shard_map/while/body/eval_jaxpr/ppermute | solution.py:17
  58.7 3.4 %collective-permute-done.1 = bf16[64,1536]{1,0:T(8,128)(2,1)} collective-permute-done((bf16[64,1536]{1,0:T(8,128)(2,1)}, bf16[64,1536]{1,0:T(8,128)(2,1)}, u32[]{:S(2)}, u32[]{:S(2)}) %collective-permute-start.1) | collective-permute-done | bytes 196640 | tf_op jit(solution)/shard_map/while/body/eval_jaxpr/ppermute | solution.py:17
  62.1 2.0 %fusion.35 = f32[1024,64]{0,1:T(8,128)S(1)} fusion(bf16[1024,1536]{1,0:T(8,128)(2,1)S(1)} %get-tuple-element.248, bf16[64,1536]{1,0:T(8,128)(2,1)} %collective-permute-done.1), kind=kOutput, calls=%fused_computation.34.clone.1 | convolution fusion | flops 201326592 | bytes 3604480 | tf_op jit(solution)/shard_map/while/body/eval_jaxpr/ak,tk->at/dot_general | solution.py:74
  71.6 3.5 %collective-permute-done = bf16[64,1536]{1,0:T(8,128)(2,1)S(1)} collective-permute-done((bf16[64,1536]{1,0:T(8,128)(2,1)}, bf16[64,1536]{1,0:T(8,128)(2,1)S(1)}, u32[]{:S(2)}, u32[]{:S(2)}) %collective-permute-start) | collective-permute-done | bytes 196640 | tf_op jit(solution)/shard_map/while/body/eval_jaxpr/ppermute | solution.py:17
  76.3 3.4 %collective-permute-done.1 = bf16[64,1536]{1,0:T(8,128)(2,1)} collective-permute-done((bf16[64,1536]{1,0:T(8,128)(2,1)}, bf16[64,1536]{1,0:T(8,128)(2,1)}, u32[]{:S(2)}, u32[]{:S(2)}) %collective-permute-start.1) | collective-permute-done | bytes 196640 | tf_op jit(solution)/shard_map/while/body/eval_jaxpr/ppermute | solution.py:17
  79.7 2.0 %fusion.35 = f32[1024,64]{0,1:T(8,128)S(1)} fusion(bf16[1024,1536]{1,0:T(8,128)(2,1)S(1)} %get-tuple-element.248, bf16[64,1536]{1,0:T(8,128)(2,1)} %collective-permute-done.1), kind=kOutput, calls=%fused_computation.34.clone.1 | convolution fusion | flops 201326592 | bytes 3604480 | tf_op jit(solution)/shard_map/while/body/eval_jaxpr/ak,tk->at/dot_general | solution.py:74
  89.3 3.5 %collective-permute-done = bf16[64,1536]{1,0:T(8,128)(2,1)S(1)} collective-permute-done((bf16[64,1536]{1,0:T(8,128)(2,1)}, bf16[64,1536]{1,0:T(8,128)(2,1)S(1)}, u32[]{:S(2)}, u32[]{:S(2)}) %collective-permute-start) | collective-permute-done | bytes 196640 | tf_op jit(solution)/shard_map/while/body/eval_jaxpr/ppermute | solution.py:17
  94.0 3.4 %collective-permute-done.1 = bf16[64,1536]{1,0:T(8,128)(2,1)} collective-permute-done((bf16[64,1536]{1,0:T(8,128)(2,1)}, bf16[64,1536]{1,0:T(8,128)(2,1)}, u32[]{:S(2)}, u32[]{:S(2)}) %collective-permute-start.1) | collective-permute-done | bytes 196640 | tf_op jit(solution)/shard_map/while/body/eval_jaxpr/ppermute | solution.py:17
  97.4 2.0 %fusion.35 = f32[1024,64]{0,1:T(8,128)S(1)} fusion(bf16[1024,1536]{1,0:T(8,128)(2,1)S(1)} %get-tuple-element.248, bf16[64,1536]{1,0:T(8,128)(2,1)} %collective-permute-done.1), kind=kOutput, calls=%fused_computation.34.clone.1 | convolution fusion | flops 201326592 | bytes 3604480 | tf_op jit(solution)/shard_map/while/body/eval_jaxpr/ak,tk->at/dot_general | solution.py:74
  106.9 3.5 %collective-permute-done = bf16[64,1536]{1,0:T(8,128)(2,1)S(1)} collective-permute-done((bf16[64,1536]{1,0:T(8,128)(2,1)}, bf16[64,1536]{1,0:T(8,128)(2,1)S(1)}, u32[]{:S(2)}, u32[]{:S(2)}) %collective-permute-start) | collective-permute-done | bytes 196640 | tf_op jit(solution)/shard_map/while/body/eval_jaxpr/ppermute | solution.py:17
  111.6 3.4 %collective-permute-done.1 = bf16[64,1536]{1,0:T(8,128)(2,1)} collective-permute-done((bf16[64,1536]{1,0:T(8,128)(2,1)}, bf16[64,1536]{1,0:T(8,128)(2,1)}, u32[]{:S(2)}, u32[]{:S(2)}) %collective-permute-start.1) | collective-permute-done | bytes 196640 | tf_op jit(solution)/shard_map/while/body/eval_jaxpr/ppermute | solution.py:17
  115.0 2.0 %fusion.35 = f32[1024,64]{0,1:T(8,128)S(1)} fusion(bf16[1024,1536]{1,0:T(8,128)(2,1)S(1)} %get-tuple-element.248, bf16[64,1536]{1,0:T(8,128)(2,1)} %collective-permute-done.1), kind=kOutput, calls=%fused_computation.34.clone.1 | convolution fusion | flops 201326592 | bytes 3604480 | tf_op jit(solution)/shard_map/while/body/eval_jaxpr/ak,tk->at/dot_general | solution.py:74
  124.6 3.5 %collective-permute-done = bf16[64,1536]{1,0:T(8,128)(2,1)S(1)} collective-permute-done((bf16[64,1536]{1,0:T(8,128)(2,1)}, bf16[64,1536]{1,0:T(8,128)(2,1)S(1)}, u32[]{:S(2)}, u32[]{:S(2)}) %collective-permute-start) | collective-permute-done | bytes 196640 | tf_op jit(solution)/shard_map/while/body/eval_jaxpr/ppermute | solution.py:17
  129.3 3.4 %collective-permute-done.1 = bf16[64,1536]{1,0:T(8,128)(2,1)} collective-permute-done((bf16[64,1536]{1,0:T(8,128)(2,1)}, bf16[64,1536]{1,0:T(8,128)(2,1)}, u32[]{:S(2)}, u32[]{:S(2)}) %collective-permute-start.1) | collective-permute-done | bytes 196640 | tf_op jit(solution)/shard_map/while/body/eval_jaxpr/ppermute | solution.py:17
  132.7 2.0 %fusion.35 = f32[1024,64]{0,1:T(8,128)S(1)} fusion(bf16[1024,1536]{1,0:T(8,128)(2,1)S(1)} %get-tuple-element.248, bf16[64,1536]{1,0:T(8,128)(2,1)} %collective-permute-done.1), kind=kOutput, calls=%fused_computation.34.clone.1 | convolution fusion | flops 201326592 | bytes 3604480 | tf_op jit(solution)/shard_map/while/body/eval_jaxpr/ak,tk->at/dot_general | solution.py:74
  142.2 3.5 %collective-permute-done = bf16[64,1536]{1,0:T(8,128)(2,1)S(1)} collective-permute-done((bf16[64,1536]{1,0:T(8,128)(2,1)}, bf16[64,1536]{1,0:T(8,128)(2,1)S(1)}, u32[]{:S(2)}, u32[]{:S(2)}) %collective-permute-start) | collective-permute-done | bytes 196640 | tf_op jit(solution)/shard_map/while/body/eval_jaxpr/ppermute | solution.py:17
  146.9 3.4 %collective-permute-done.1 = bf16[64,1536]{1,0:T(8,128)(2,1)} collective-permute-done((bf16[64,1536]{1,0:T(8,128)(2,1)}, bf16[64,1536]{1,0:T(8,128)(2,1)}, u32[]{:S(2)}, u32[]{:S(2)}) %collective-permute-start.1) | collective-permute-done | bytes 196640 | tf_op jit(solution)/shard_map/while/body/eval_jaxpr/ppermute | solution.py:17
  150.3 2.0 %fusion.35 = f32[1024,64]{0,1:T(8,128)S(1)} fusion(bf16[1024,1536]{1,0:T(8,128)(2,1)S(1)} %get-tuple-element.248, bf16[64,1536]{1,0:T(8,128)(2,1)} %collective-permute-done.1), kind=kOutput, calls=%fused_computation.34.clone.1 | convolution fusion | flops 201326592 | bytes 3604480 | tf_op jit(solution)/shard_map/while/body/eval_jaxpr/ak,tk->at/dot_general | solution.py:74
  159.9 3.5 %collective-permute-done.2 = bf16[64,1536]{1,0:T(8,128)(2,1)S(1)} collective-permute-done((bf16[64,1536]{1,0:T(8,128)(2,1)}, bf16[64,1536]{1,0:T(8,128)(2,1)S(1)}, u32[]{:S(2)}, u32[]{:S(2)}) %collective-permute-start.2) | collective-permute-done | bytes 196640 | tf_op jit(solution)/shard_map/ppermute | solution.py:17
  163.4 2.5 %fusion.14 = f32[1024,64]{0,1:T(8,128)S(1)} fusion(bf16[64,1536]{1,0:T(8,128)(2,1)S(1)} %collective-permute-done.2, bf16[1024,1536]{0,1:T(8,128)(2,1)} %reshape.233), kind=kOutput, calls=%fused_computation.36 | convolution fusion | flops 201326592 | bytes 3604480 | tf_op jit(solution)/shard_map/ak,tk->at/dot_general | solution.py:74
  166.8 3.8 %copy.12 = f32[8,64,1024]{2,1,0:T(8,128)} copy(f32[8,64,1024]{1,0,2:T(8,128)} %bitcast.42) | data formatting | bytes 4194304 | tf_op jit(solution)/shard_map/reshape | solution.py:104
  (114 shorter events, 69.0 us)
Async XLA Ops:
  28.9 1.9 %copy-start.1 = (f32[16,8,64,64]{2,1,3,0:T(8,128)}, f32[16,8,64,64]{2,1,3,0:T(8,128)S(1)}, u32[]{:S(2)}) copy-start(f32[16,8,64,64]{2,1,3,0:T(8,128)S(1)} %constant_dynamic-update-slice_fusion.3) | copy-start | bytes 6291460
  30.8 9.0 %collective-permute-start = (bf16[64,1536]{1,0:T(8,128)(2,1)}, bf16[64,1536]{1,0:T(8,128)(2,1)S(1)}, u32[]{:S(2)}, u32[]{:S(2)}) collective-permute-start(bf16[64,1536]{1,0:T(8,128)(2,1)} %get-tuple-element.235), channel_id=1, source_target_pairs={{0,15},{1,0},{2,1},{3,2},{4,3},{5,4},{6,5},{7,6},{8,7},{9,8},{10,9... | collective-permute-start | bytes 589832 | tf_op jit(solution)/shard_map/while/body/eval_jaxpr/ppermute | solution.py:17
  36.3 8.1 %collective-permute-start.1 = (bf16[64,1536]{1,0:T(8,128)(2,1)}, bf16[64,1536]{1,0:T(8,128)(2,1)}, u32[]{:S(2)}, u32[]{:S(2)}) collective-permute-start(bf16[64,1536]{1,0:T(8,128)(2,1)} %get-tuple-element.236), channel_id=1, source_target_pairs={{0,1},{1,2},{2,3},{3,4},{4,5},{5,6},{6,7},{7,8},{8,9},{9,10},{10,1... | collective-permute-start | bytes 589832 | tf_op jit(solution)/shard_map/while/body/eval_jaxpr/ppermute | solution.py:17
  39.8 1.1 copy-start
  52.8 4.6 %collective-permute-start = (bf16[64,1536]{1,0:T(8,128)(2,1)}, bf16[64,1536]{1,0:T(8,128)(2,1)S(1)}, u32[]{:S(2)}, u32[]{:S(2)}) collective-permute-start(bf16[64,1536]{1,0:T(8,128)(2,1)} %get-tuple-element.235), channel_id=1, source_target_pairs={{0,15},{1,0},{2,1},{3,2},{4,3},{5,4},{6,5},{7,6},{8,7},{9,8},{10,9... | collective-permute-start | bytes 589832 | tf_op jit(solution)/shard_map/while/body/eval_jaxpr/ppermute | solution.py:17
  54.0 8.1 %collective-permute-start.1 = (bf16[64,1536]{1,0:T(8,128)(2,1)}, bf16[64,1536]{1,0:T(8,128)(2,1)}, u32[]{:S(2)}, u32[]{:S(2)}) collective-permute-start(bf16[64,1536]{1,0:T(8,128)(2,1)} %get-tuple-element.236), channel_id=1, source_target_pairs={{0,1},{1,2},{2,3},{3,4},{4,5},{5,6},{6,7},{7,8},{8,9},{9,10},{10,1... | collective-permute-start | bytes 589832 | tf_op jit(solution)/shard_map/while/body/eval_jaxpr/ppermute | solution.py:17
  57.5 1.1 copy-start
  70.5 4.6 %collective-permute-start = (bf16[64,1536]{1,0:T(8,128)(2,1)}, bf16[64,1536]{1,0:T(8,128)(2,1)S(1)}, u32[]{:S(2)}, u32[]{:S(2)}) collective-permute-start(bf16[64,1536]{1,0:T(8,128)(2,1)} %get-tuple-element.235), channel_id=1, source_target_pairs={{0,15},{1,0},{2,1},{3,2},{4,3},{5,4},{6,5},{7,6},{8,7},{9,8},{10,9... | collective-permute-start | bytes 589832 | tf_op jit(solution)/shard_map/while/body/eval_jaxpr/ppermute | solution.py:17
  71.6 8.1 %collective-permute-start.1 = (bf16[64,1536]{1,0:T(8,128)(2,1)}, bf16[64,1536]{1,0:T(8,128)(2,1)}, u32[]{:S(2)}, u32[]{:S(2)}) collective-permute-start(bf16[64,1536]{1,0:T(8,128)(2,1)} %get-tuple-element.236), channel_id=1, source_target_pairs={{0,1},{1,2},{2,3},{3,4},{4,5},{5,6},{6,7},{7,8},{8,9},{9,10},{10,1... | collective-permute-start | bytes 589832 | tf_op jit(solution)/shard_map/while/body/eval_jaxpr/ppermute | solution.py:17
  75.1 1.1 copy-start
  88.1 4.6 %collective-permute-start = (bf16[64,1536]{1,0:T(8,128)(2,1)}, bf16[64,1536]{1,0:T(8,128)(2,1)S(1)}, u32[]{:S(2)}, u32[]{:S(2)}) collective-permute-start(bf16[64,1536]{1,0:T(8,128)(2,1)} %get-tuple-element.235), channel_id=1, source_target_pairs={{0,15},{1,0},{2,1},{3,2},{4,3},{5,4},{6,5},{7,6},{8,7},{9,8},{10,9... | collective-permute-start | bytes 589832 | tf_op jit(solution)/shard_map/while/body/eval_jaxpr/ppermute | solution.py:17
  89.3 8.1 %collective-permute-start.1 = (bf16[64,1536]{1,0:T(8,128)(2,1)}, bf16[64,1536]{1,0:T(8,128)(2,1)}, u32[]{:S(2)}, u32[]{:S(2)}) collective-permute-start(bf16[64,1536]{1,0:T(8,128)(2,1)} %get-tuple-element.236), channel_id=1, source_target_pairs={{0,1},{1,2},{2,3},{3,4},{4,5},{5,6},{6,7},{7,8},{8,9},{9,10},{10,1... | collective-permute-start | bytes 589832 | tf_op jit(solution)/shard_map/while/body/eval_jaxpr/ppermute | solution.py:17
  92.8 1.1 copy-start
  105.8 4.6 %collective-permute-start = (bf16[64,1536]{1,0:T(8,128)(2,1)}, bf16[64,1536]{1,0:T(8,128)(2,1)S(1)}, u32[]{:S(2)}, u32[]{:S(2)}) collective-permute-start(bf16[64,1536]{1,0:T(8,128)(2,1)} %get-tuple-element.235), channel_id=1, source_target_pairs={{0,15},{1,0},{2,1},{3,2},{4,3},{5,4},{6,5},{7,6},{8,7},{9,8},{10,9... | collective-permute-start | bytes 589832 | tf_op jit(solution)/shard_map/while/body/eval_jaxpr/ppermute | solution.py:17
  106.9 8.1 %collective-permute-start.1 = (bf16[64,1536]{1,0:T(8,128)(2,1)}, bf16[64,1536]{1,0:T(8,128)(2,1)}, u32[]{:S(2)}, u32[]{:S(2)}) collective-permute-start(bf16[64,1536]{1,0:T(8,128)(2,1)} %get-tuple-element.236), channel_id=1, source_target_pairs={{0,1},{1,2},{2,3},{3,4},{4,5},{5,6},{6,7},{7,8},{8,9},{9,10},{10,1... | collective-permute-start | bytes 589832 | tf_op jit(solution)/shard_map/while/body/eval_jaxpr/ppermute | solution.py:17
  110.4 1.1 copy-start
  123.5 4.6 %collective-permute-start = (bf16[64,1536]{1,0:T(8,128)(2,1)}, bf16[64,1536]{1,0:T(8,128)(2,1)S(1)}, u32[]{:S(2)}, u32[]{:S(2)}) collective-permute-start(bf16[64,1536]{1,0:T(8,128)(2,1)} %get-tuple-element.235), channel_id=1, source_target_pairs={{0,15},{1,0},{2,1},{3,2},{4,3},{5,4},{6,5},{7,6},{8,7},{9,8},{10,9... | collective-permute-start | bytes 589832 | tf_op jit(solution)/shard_map/while/body/eval_jaxpr/ppermute | solution.py:17
  124.6 8.1 %collective-permute-start.1 = (bf16[64,1536]{1,0:T(8,128)(2,1)}, bf16[64,1536]{1,0:T(8,128)(2,1)}, u32[]{:S(2)}, u32[]{:S(2)}) collective-permute-start(bf16[64,1536]{1,0:T(8,128)(2,1)} %get-tuple-element.236), channel_id=1, source_target_pairs={{0,1},{1,2},{2,3},{3,4},{4,5},{5,6},{6,7},{7,8},{8,9},{9,10},{10,1... | collective-permute-start | bytes 589832 | tf_op jit(solution)/shard_map/while/body/eval_jaxpr/ppermute | solution.py:17
  128.1 1.1 copy-start
  141.1 4.6 %collective-permute-start = (bf16[64,1536]{1,0:T(8,128)(2,1)}, bf16[64,1536]{1,0:T(8,128)(2,1)S(1)}, u32[]{:S(2)}, u32[]{:S(2)}) collective-permute-start(bf16[64,1536]{1,0:T(8,128)(2,1)} %get-tuple-element.235), channel_id=1, source_target_pairs={{0,15},{1,0},{2,1},{3,2},{4,3},{5,4},{6,5},{7,6},{8,7},{9,8},{10,9... | collective-permute-start | bytes 589832 | tf_op jit(solution)/shard_map/while/body/eval_jaxpr/ppermute | solution.py:17
  142.2 8.1 %collective-permute-start.1 = (bf16[64,1536]{1,0:T(8,128)(2,1)}, bf16[64,1536]{1,0:T(8,128)(2,1)}, u32[]{:S(2)}, u32[]{:S(2)}) collective-permute-start(bf16[64,1536]{1,0:T(8,128)(2,1)} %get-tuple-element.236), channel_id=1, source_target_pairs={{0,1},{1,2},{2,3},{3,4},{4,5},{5,6},{6,7},{7,8},{8,9},{9,10},{10,1... | collective-permute-start | bytes 589832 | tf_op jit(solution)/shard_map/while/body/eval_jaxpr/ppermute | solution.py:17
  145.7 1.1 copy-start
  158.8 4.6 %collective-permute-start.2 = (bf16[64,1536]{1,0:T(8,128)(2,1)}, bf16[64,1536]{1,0:T(8,128)(2,1)S(1)}, u32[]{:S(2)}, u32[]{:S(2)}) collective-permute-start(bf16[64,1536]{1,0:T(8,128)(2,1)} %get-tuple-element.162), channel_id=1, source_target_pairs={{0,15},{1,0},{2,1},{3,2},{4,3},{5,4},{6,5},{7,6},{8,7},{9,8},{10,9... | collective-permute-start | bytes 589832 | tf_op jit(solution)/shard_map/ppermute | solution.py:17
where the time goes:
time: 172 us; the launch traced here: 171 us
  local copies, waits for them, and re-layouts  69 us (40%)
  waiting for transfers between devices  51.8 us (30%)
  matrix products  27.6 us (16%)
  starting transfers between devices  13.2 us (8%)
  other arithmetic  8.51 us (5%)
    ppermute x15, waiting for transfers between devices, from_behind(): lax.ppermute(array, axis, [(i, (i + by) % size) for i in range(size)])  51.8 us
    dot_general x16, matrix products, correlate(): jnp.einsum('ak,tk->at', modulated, other, preferred_element_type=jnp.floa...  27 us
    while x28, local copies, waits for them, and re-layouts  22.7 us
    dynamic_update_slice x16, local copies, waits for them, and re-layouts, deposit(): lax.dynamic_update_slice(tiles, product[None], (slot, zero, zero, zero))  17.4 us
    ppermute x15, starting transfers between devices, from_behind(): lax.ppermute(array, axis, [(i, (i + by) % size) for i in range(size)])  13.2 us
    reshape x1, local copies, waits for them, and re-layouts, modulate(): return stacked.reshape(2 * lag_count * members, 2 * win_count * bin_count)  9.4 us
    sub x7, local copies, waits for them, and re-layouts, advance_two(): tiles = deposit(tiles, back_sums[0] - back_sums[1], cycle_size - offset)  5.63 us
    unnamed x4, local copies, waits for them, and re-layouts  4.7 us
  transfers between devices with their start and end apart: 15, of which 15 were waited for; matrix products, arithmetic and copies ran while one was open for 5% of the time, Pallas kernels for 0%

commit v1 on v0

v1 whole, which is shorter than its diff:
```python
import functools
import math

import jax
import jax.numpy as jnp
import numpy as np
from jax import lax
from jax.experimental import pallas as pl
from jax.experimental.pallas import tpu as pltpu
from jax.sharding import PartitionSpec as P

LAGS = 8
LANES = 128
level_floor = 0.3
first_bin = 96.0
reach = 2


def phase_tables(bin_count, lag_count, scale):
    freq = first_bin + np.arange(bin_count, dtype=np.float32)
    shifts = 3.0 + 5.0 * np.arange(lag_count, dtype=np.float32)
    theta = np.float32(2.0 * math.pi) * freq[None, :] * shifts[:, None] / np.float32(512.0)
    tables = np.stack([np.cos(theta), np.sin(theta)]) * np.float32(scale)
    return np.tile(tables, (1, 1, LANES // bin_count)).astype(np.float32)


def kernel(
    devices, spectra, gaps, tables, out, blocks, modulated,
    ring_send, ring_recv, pair_send, pair_recv,
):
    members, length = spectra.shape[1], spectra.shape[2]
    windows = gaps.shape[0]
    bins = length // windows
    lag_count = out.shape[0]
    half = members // 2
    chips = devices // 2
    far = chips // 2
    turn = (chips + 1) // 2

    me = lax.axis_index("blk")
    chip, core = me // 2, me % 2
    spot = jnp.where(chip % 2 == 0, chip // 2, chips - 1 - chip // 2)

    def chip_at(position):
        position = (position + 2 * chips) % chips
        return jnp.where(position < turn, 2 * position, 2 * chips - 1 - 2 * position)

    targets = (chip_at(spot + 1) * 2 + core, chip_at(spot - 1) * 2 + core)
    partner = chip * 2 + (1 - core)

    def source_chip(way, distance):
        return chip_at(spot - distance if way == 0 else spot + distance)

    def piece(block, h):
        return blocks.at[block, pl.ds(h * half, half), :]

    def ring(way, step, h, incoming=False):
        place = piece(source_chip(way, step + 1 if incoming else step) * 2 + core, h)
        return pltpu.make_async_remote_copy(
            src_ref=place, dst_ref=place,
            send_sem=ring_send.at[way, step, h], recv_sem=ring_recv.at[way, step, h],
            device_id={"blk": targets[way]}, device_id_type=pl.DeviceIdType.MESH,
        )

    def pair(way, distance, h, incoming=False):
        side = 1 - core if incoming else core
        place = piece(source_chip(way, distance) * 2 + side, h)
        return pltpu.make_async_remote_copy(
            src_ref=place, dst_ref=place,
            send_sem=pair_send.at[way, distance, h], recv_sem=pair_recv.at[way, distance, h],
            device_id={"blk": partner}, device_id_type=pl.DeviceIdType.MESH,
        )

    barrier = pltpu.get_barrier_semaphore()
    for other in (*targets, partner):
        pl.semaphore_signal(
            barrier, inc=1, device_id={"blk": other}, device_id_type=pl.DeviceIdType.MESH
        )

    window_of = lax.broadcasted_iota(jnp.int32, (windows, length), 1) // bins
    spread = window_of == lax.broadcasted_iota(jnp.int32, (windows, length), 0)
    live = lax.dot_general(
        gaps[...].astype(jnp.float32).astype(jnp.bfloat16),
        spread.astype(jnp.float32).astype(jnp.bfloat16),
        (((0,), (0,)), ((), ())),
        preferred_element_type=jnp.float32,
    )
    bin_of = lax.broadcasted_iota(jnp.int32, (members, LANES), 1) % bins
    count = 1 + jnp.minimum(bin_of, reach) + jnp.minimum(bins - 1 - bin_of, reach)
    weight = 1.0 / count.astype(jnp.float32)
    for at in range(0, length, LANES):
        cut = slice(at, at + LANES)
        real = spectra[0, :, cut].astype(jnp.float32)
        imag = spectra[1, :, cut].astype(jnp.float32)
        amplitude = jnp.sqrt(real * real + imag * imag)
        total = amplitude
        for off in range(1, reach + 1):
            total += jnp.where(bin_of >= off, pltpu.roll(amplitude, off, 1), 0.0)
            total += jnp.where(bin_of < bins - off, pltpu.roll(amplitude, LANES - off, 1), 0.0)
        level = jnp.maximum(total * weight, level_floor)
        factor = live[:, cut] / level
        blocks[me, :, at : at + LANES] = (real * factor).astype(jnp.bfloat16)
        blocks[me, :, length + at : length + at + LANES] = (imag * factor).astype(jnp.bfloat16)

    pl.semaphore_wait(barrier, 3)

    for h in (0, 1):
        ring(0, 0, h).start()
        ring(1, 0, 1 - h).start()
    for h in (0, 1):
        pair(0, 0, h).start()

    def modulate(lag, carry):
        cosine = tables[0, pl.ds(lag, 1), :]
        sine = tables[1, pl.ds(lag, 1), :]
        rows = pl.ds(pl.multiple_of(lag * members, members), members)
        for at in range(0, length, LANES):
            real = blocks[me, :, at : at + LANES].astype(jnp.float32)
            imag = blocks[me, :, length + at : length + at + LANES].astype(jnp.float32)
            modulated[rows, at : at + LANES] = (cosine * real - sine * imag).astype(jnp.bfloat16)
            modulated[rows, length + at : length + at + LANES] = (
                cosine * imag + sine * real
            ).astype(jnp.bfloat16)
        return carry

    lax.fori_loop(0, lag_count, modulate, 0)

    def correlate(way, distance):
        tile = source_chip(way, distance)
        others = blocks[pl.ds(tile * 2, 2)].reshape(2 * members, 2 * length)
        sums = lax.dot_general(
            modulated[...], others, (((1,), (1,)), ((), ())),
            preferred_element_type=jnp.float32,
        )
        width = 2 * members
        columns = pl.ds(pl.multiple_of(tile * width, width), width)
        out[:, :, columns] = sums.reshape(lag_count, members, width)

    def pair_ready(way, distance):
        for h in (0, 1):
            pair(way, distance, h, incoming=True).wait_recv()

    def take(step, h, last):
        for way in (0, 1):
            part = h if way == 0 else 1 - h
            ring(way, step - 1, part, incoming=True).wait_recv()
            if not last or h == 0:
                ring(way, step, part).start()
            pair(way, step, part).start()

    take(1, 0, far == 2)
    pair_ready(0, 0)
    correlate(0, 0)
    take(1, 1, far == 2)

    def onward(step, last):
        take(step, 0, last)
        pair_ready(0, step - 1)
        correlate(0, step - 1)
        take(step, 1, last)
        pair_ready(1, step - 1)
        correlate(1, step - 1)

    def body(step, carry):
        onward(step, False)
        return carry

    lax.fori_loop(2, far - 1, body, 0)
    onward(far - 1, True)

    pair_ready(0, far - 1)
    correlate(0, far - 1)
    pair_ready(1, far - 1)
    for way in (0, 1):
        ring(way, far - 1, way, incoming=True).wait_recv()
        pair(way, far, way).start()
    correlate(1, far - 1)
    for way in (0, 1):
        pair(way, far, way, incoming=True).wait_recv()
    correlate(0, far)

    def drain(step, carry):
        for way in (0, 1):
            for h in (0, 1):
                ring(way, step, h).wait_send()
                pair(way, step + 1, h).wait_send()
        return carry

    lax.fori_loop(0, far - 1, drain, 0)
    for way in (0, 1):
        ring(way, far - 1, way).wait_send()
        pair(way, far, way).wait_send()
    for h in (0, 1):
        pair(0, 0, h).wait_send()


def per_device(spectra, gap_mask):
    devices = lax.axis_size("blk")
    members, length = spectra.shape[1], spectra.shape[2]
    far = devices // 4
    tables = phase_tables(length // gap_mask.shape[1], LAGS, 1.0 / math.sqrt(length))
    return pl.pallas_call(
        functools.partial(kernel, devices),
        out_shape=jax.ShapeDtypeStruct((LAGS, members, devices * members), jnp.float32),
        in_specs=[pl.BlockSpec(memory_space=pltpu.VMEM)] * 3,
        out_specs=pl.BlockSpec(memory_space=pltpu.VMEM),
        scratch_shapes=[
            pltpu.VMEM((devices, members, 2 * length), jnp.bfloat16),
            pltpu.VMEM((LAGS * members, 2 * length), jnp.bfloat16),
            pltpu.SemaphoreType.DMA((2, far, 2)),
            pltpu.SemaphoreType.DMA((2, far, 2)),
            pltpu.SemaphoreType.DMA((2, far + 1, 2)),
            pltpu.SemaphoreType.DMA((2, far + 1, 2)),
        ],
        compiler_params=pltpu.CompilerParams(
            collective_id=0, has_side_effects=True, vmem_limit_bytes=60 * 1024 * 1024
        ),
    )(spectra, gap_mask.T, jnp.asarray(tables))


def solution(mesh):
    placed = (P(None, ("group", "blk"), None), P(("group", "blk"), None))
    return jax.shard_map(
        per_device,
        mesh=mesh,
        in_specs=placed,
        out_specs=P(None, ("group", "blk"), None),
        check_vma=False,
    )
```

time: 172 us -> 29.6 us (0.17)
  local copies, waits for them, and re-layouts: 69 us -> 3.16 us
  waiting for transfers between devices: 51.8 us -> 0 us
  matrix products: 27.6 us -> 0 us
  Pallas kernels: 0 us -> 26.3 us
  starting transfers between devices: 13.2 us -> 0 us
  other arithmetic: 8.51 us -> 0 us
    ppermute x15 -> x0, waiting for transfers between devices: 51.8 us -> none  [from_behind(): lax.ppermute(array, axis, [(i, (i + by) % size) for i in range(size)])]
    dot_general x17 -> x0, matrix products: 27.6 us -> none  [the longest x16 27 us: correlate(): jnp.einsum('ak,tk->at', modulated, other, preferred_element_type=jnp.floa...]
    while x30 -> x0, local copies, waits for them, and re-layouts: 26.7 us -> none
    pallas_call x0 -> x1, Pallas kernels: none -> 26.3 us  [per_device(): pl.pallas_call(functools.partial(kernel, devices), out_shape=jax.ShapeDty...]
    dynamic_update_slice x16 -> x0, local copies, waits for them, and re-layouts: 17.4 us -> none  [deposit(): lax.dynamic_update_slice(tiles, product[None], (slot, zero, zero, zero))]
    ppermute x15 -> x0, starting transfers between devices: 13.2 us -> none  [from_behind(): lax.ppermute(array, axis, [(i, (i + by) % size) for i in range(size)])]
    reshape x2 -> x0, local copies, waits for them, and re-layouts: 13.2 us -> none  [the longest x1 9.4 us: modulate(): return stacked.reshape(2 * lag_count * members, 2 * win_count * bin_count)]
    sub x16 -> x0, local copies, waits for them, and re-layouts: 6.55 us -> none  [the longest x7 5.63 us: advance_two(): tiles = deposit(tiles, back_sums[0] - back_sums[1], cycle_size - offset)]
  transfers between devices with their start and end apart: 15 -> 0, of which waited for: 15 -> 0; matrix products, arithmetic and copies ran while one was open for 5% -> 0% of each run, Pallas kernels for 0% -> 0%
where the time goes in v1:
time: 29.6 us; the launch traced here: 29.4 us
  Pallas kernels  26.3 us (89%)
  local copies, waits for them, and re-layouts  3.16 us (11%)
    pallas_call x1, Pallas kernels, per_device(): pl.pallas_call(functools.partial(kernel, devices), out_shape=jax.ShapeDty...  26.3 us
    unnamed x1, local copies, waits for them, and re-layouts  3.16 us

profile of v1, /device:TPU:0, one launch (start us, length us, event | category | flops | bytes accessed | tf_op | source)
XLA Modules:
  0.0 29.4 jit_solution(15660091312896101106)
XLA Ops:
  0.0 26.3 %shard_map.37 = f32[8,64,1024]{2,1,0:T(8,128)} custom-call(bf16[2,64,768]{2,1,0:T(8,128)(2,1)} %spectra.1, s32[48,64]{1,0:T(8,128)} %bitcast.1, f32[2,8,128]{2,1,0:T(8,128)} %constant.2.clone.tables), custom_call_target="tpu_custom_call" | custom-call | tf_op jit(solution)/shard_map/pallas_call | solution.py:202
  26.3 3.2 %copy.5 = f32[8,64,1024]{2,1,0:T(8,128)} copy(f32[8,64,1024]{2,1,0:T(8,128)} %shard_map.37) | data formatting | bytes 4194304

commit v2 on v1

--- a/solution.py
+++ b/solution.py
@@ -22,6 +22,54 @@
     theta = np.float32(2.0 * math.pi) * freq[None, :] * shifts[:, None] / np.float32(512.0)
     tables = np.stack([np.cos(theta), np.sin(theta)]) * np.float32(scale)
     return np.tile(tables, (1, 1, LANES // bin_count)).astype(np.float32)
+
+
+def ring_chip(chips, position):
+    position = (position + 2 * chips) % chips
+    return jnp.where(position < (chips + 1) // 2, 2 * position, 2 * chips - 1 - 2 * position)
+
+
+def ring_spot(chips, chip):
+    return jnp.where(chip % 2 == 0, chip // 2, chips - 1 - chip // 2)
+
+
+def tile_product(modulated, blocks, tile, lag_count):
+    _, members, depth = blocks.shape
+    others = blocks[pl.ds(tile * 2, 2)].reshape(2 * members, depth)
+    sums = lax.dot_general(
+        modulated[...], others, (((1,), (1,)), ((), ())), preferred_element_type=jnp.float32
+    )
+    return sums.reshape(lag_count, members, 2 * members)
+
+
+def finish(devices, partial, blocks, modulated, out, last, done):
+    chips = devices // 2
+    lag_count, members = partial.shape[0], partial.shape[1]
+    width = 2 * members
+    spot = ring_spot(chips, lax.axis_index("blk") // 2)
+    far_tile = ring_chip(chips, spot + chips // 2)
+
+    def columns(tile):
+        return pl.ds(pl.multiple_of(tile * width, width), width)
+
+    def place(away):
+        cut = columns(ring_chip(chips, spot + chips // 2 + away))
+        return pltpu.make_async_copy(partial.at[:, :, cut], out.at[:, :, cut], done.at[away])
+
+    def begin(away, carry):
+        place(away).start()
+        return carry
+
+    def end(away, carry):
+        place(away).wait()
+        return carry
+
+    lax.fori_loop(1, chips, begin, 0)
+    last[...] = tile_product(modulated, blocks, far_tile, lag_count)
+    tail = pltpu.make_async_copy(last, out.at[:, :, columns(far_tile)], done.at[0])
+    tail.start()
+    lax.fori_loop(1, chips, end, 0)
+    tail.wait()
 
 
 def kernel(
@@ -35,15 +83,13 @@
     half = members // 2
     chips = devices // 2
     far = chips // 2
-    turn = (chips + 1) // 2
 
     me = lax.axis_index("blk")
     chip, core = me // 2, me % 2
-    spot = jnp.where(chip % 2 == 0, chip // 2, chips - 1 - chip // 2)
+    spot = ring_spot(chips, chip)
 
     def chip_at(position):
-        position = (position + 2 * chips) % chips
-        return jnp.where(position < turn, 2 * position, 2 * chips - 1 - 2 * position)
+        return ring_chip(chips, position)
 
     targets = (chip_at(spot + 1) * 2 + core, chip_at(spot - 1) * 2 + core)
     partner = chip * 2 + (1 - core)
@@ -127,14 +173,9 @@
 
     def correlate(way, distance):
         tile = source_chip(way, distance)
-        others = blocks[pl.ds(tile * 2, 2)].reshape(2 * members, 2 * length)
-        sums = lax.dot_general(
-            modulated[...], others, (((1,), (1,)), ((), ())),
-            preferred_element_type=jnp.float32,
-        )
         width = 2 * members
         columns = pl.ds(pl.multiple_of(tile * width, width), width)
-        out[:, :, columns] = sums.reshape(lag_count, members, width)
+        out[:, :, columns] = tile_product(modulated, blocks, tile, lag_count)
 
     def pair_ready(way, distance):
         for h in (0, 1):
@@ -177,7 +218,6 @@
     correlate(1, far - 1)
     for way in (0, 1):
         pair(way, far, way, incoming=True).wait_recv()
-    correlate(0, far)
 
     def drain(step, carry):
         for way in (0, 1):
@@ -199,23 +239,38 @@
     members, length = spectra.shape[1], spectra.shape[2]
     far = devices // 4
     tables = phase_tables(length // gap_mask.shape[1], LAGS, 1.0 / math.sqrt(length))
-    return pl.pallas_call(
+    result = (LAGS, members, devices * members)
+    vmem = pl.BlockSpec(memory_space=pltpu.VMEM)
+    partial, blocks, modulated = pl.pallas_call(
         functools.partial(kernel, devices),
-        out_shape=jax.ShapeDtypeStruct((LAGS, members, devices * members), jnp.float32),
-        in_specs=[pl.BlockSpec(memory_space=pltpu.VMEM)] * 3,
-        out_specs=pl.BlockSpec(memory_space=pltpu.VMEM),
-        scratch_shapes=[
+        out_shape=[
+            pltpu.VMEM(result, jnp.float32),
             pltpu.VMEM((devices, members, 2 * length), jnp.bfloat16),
             pltpu.VMEM((LAGS * members, 2 * length), jnp.bfloat16),
+        ],
+        in_specs=[vmem] * 3,
+        out_specs=[vmem] * 3,
+        scratch_shapes=[
             pltpu.SemaphoreType.DMA((2, far, 2)),
             pltpu.SemaphoreType.DMA((2, far, 2)),
             pltpu.SemaphoreType.DMA((2, far + 1, 2)),
             pltpu.SemaphoreType.DMA((2, far + 1, 2)),
         ],
         compiler_params=pltpu.CompilerParams(
-            collective_id=0, has_side_effects=True, vmem_limit_bytes=60 * 1024 * 1024
+            collective_id=0, has_side_effects=True, vmem_limit_bytes=16 * 1024 * 1024
         ),
     )(spectra, gap_mask.T, jnp.asarray(tables))
+    return pl.pallas_call(
+        functools.partial(finish, devices),
+        out_shape=jax.ShapeDtypeStruct(result, jnp.float32),
+        in_specs=[vmem] * 3,
+        out_specs=pl.BlockSpec(memory_space=pl.ANY),
+        scratch_shapes=[
+            pltpu.VMEM((LAGS, members, 2 * members), jnp.float32),
+            pltpu.SemaphoreType.DMA((devices // 2,)),
+        ],
+        compiler_params=pltpu.CompilerParams(vmem_limit_bytes=16 * 1024 * 1024),
+    )(partial, blocks, modulated)
 
 
 def solution(mesh):

time: 29.6 us -> 27.1 us (0.916)
  Pallas kernels: 26.3 us -> 24.5 us
  local copies, waits for them, and re-layouts: 3.16 us -> 2.36 us
    pallas_call x1 -> x2, Pallas kernels: 26.3 us -> 24.5 us  [the longest x1 23 us: per_device(): pl.pallas_call(functools.partial(kernel, devices), out_shape=[pltpu.VMEM(...]
    unnamed x1 -> x6, local copies, waits for them, and re-layouts: 3.16 us -> 2.36 us
where the time goes in v2:
time: 27.1 us; the launch traced here: 26.8 us
  Pallas kernels  24.5 us (90%)
  local copies, waits for them, and re-layouts  2.36 us (9%)
    pallas_call x1, Pallas kernels, per_device(): pl.pallas_call(functools.partial(kernel, devices), out_shape=[pltpu.VMEM(...  23 us
    unnamed x6, local copies, waits for them, and re-layouts  2.36 us
    pallas_call x1, Pallas kernels, per_device(): pl.pallas_call(functools.partial(finish, devices), out_shape=jax.ShapeDty...  1.44 us

profile of v2, /device:TPU:0, one launch (start us, length us, event | category | flops | bytes accessed | tf_op | source)
XLA Modules:
  0.0 26.8 jit_solution(5474535137169578592)
XLA Ops:
  0.0 0.0 copy-start
  0.0 0.9 %copy-done = bf16[2,64,768]{2,1,0:T(8,128)(2,1)S(1)} copy-done((bf16[2,64,768]{2,1,0:T(8,128)(2,1)S(1)}, bf16[2,64,768]{2,1,0:T(8,128)(2,1)}, u32[]{:S(2)}) %copy-start) | copy-done | bytes 196632
  0.9 0.0 copy-start.1
  0.9 0.7 %copy-done.1 = s32[64,48]{0,1:T(8,128)S(1)} copy-done((s32[64,48]{0,1:T(8,128)S(1)}, s32[64,48]{0,1:T(8,128)}, u32[]{:S(2)}) %copy-start.1) | copy-done | bytes 12312
  1.7 0.0 copy-start.2
  1.7 0.7 %copy-done.2 = f32[2,8,128]{2,1,0:T(8,128)S(1)} copy-done((f32[2,8,128]{2,1,0:T(8,128)S(1)}, f32[2,8,128]{2,1,0:T(8,128)}, u32[]{:S(2)}) %copy-start.2) | copy-done | bytes 8216
  2.4 23.0 %shard_map.37 = (f32[8,64,1024]{2,1,0:T(8,128)S(1)}, bf16[16,64,1536]{2,1,0:T(8,128)(2,1)S(1)}, bf16[512,1536]{1,0:T(8,128)(2,1)S(1)}) custom-call(bf16[2,64,768]{2,1,0:T(8,128)(2,1)S(1)} %copy-done, s32[48,64]{1,0:T(8,128)S(1)} %bitcast.1, f32[2,8,128]{2,1,0:T(8,128)S(1)} %copy-done.2), custom_call_target="tpu_custom_call" | custom-call | tf_op jit(solution)/shard_map/pallas_call | solution.py:244
  25.4 1.4 %shard_map.38 = f32[8,64,1024]{2,1,0:T(8,128)} custom-call(f32[8,64,1024]{2,1,0:T(8,128)S(1)} %get-tuple-element.8.partial, bf16[16,64,1536]{2,1,0:T(8,128)(2,1)S(1)} %get-tuple-element.9.blocks, bf16[512,1536]{1,0:T(8,128)(2,1)S(1)} %get-tuple-element.10.modulated), custom_call_target="tpu_custom_call" | custom-call | tf_op jit(solution)/shard_map/pallas_call | solution.py:263
Async XLA Ops:
  0.0 0.9 %copy-start = (bf16[2,64,768]{2,1,0:T(8,128)(2,1)S(1)}, bf16[2,64,768]{2,1,0:T(8,128)(2,1)}, u32[]{:S(2)}) copy-start(bf16[2,64,768]{2,1,0:T(8,128)(2,1)} %spectra.1) | copy-start | bytes 589828
  0.9 0.7 %copy-start.1 = (s32[64,48]{0,1:T(8,128)S(1)}, s32[64,48]{0,1:T(8,128)}, u32[]{:S(2)}) copy-start(s32[64,48]{0,1:T(8,128)} %param.4) | copy-start | bytes 36868
  1.7 0.7 %copy-start.2 = (f32[2,8,128]{2,1,0:T(8,128)S(1)}, f32[2,8,128]{2,1,0:T(8,128)}, u32[]{:S(2)}) copy-start(f32[2,8,128]{2,1,0:T(8,128)} %constant.2.clone.tables) | copy-start | bytes 24580

commit v3 on v2

--- a/solution.py
+++ b/solution.py
@@ -73,8 +73,8 @@
 
 
 def kernel(
-    devices, spectra, gaps, tables, out, blocks, modulated,
-    ring_send, ring_recv, pair_send, pair_recv,
+    devices, spectra_in, gaps_in, tables_in, out, blocks, modulated,
+    spectra, gaps, tables, fetched, ring_send, ring_recv, pair_send, pair_recv,
 ):
     members, length = spectra.shape[1], spectra.shape[2]
     windows = gaps.shape[0]
@@ -117,6 +117,15 @@
             device_id={"blk": partner}, device_id_type=pl.DeviceIdType.MESH,
         )
 
+    fetches = [
+        pltpu.make_async_copy(source, place, fetched.at[i])
+        for i, (source, place) in enumerate(
+            ((gaps_in, gaps), (spectra_in, spectra), (tables_in, tables))
+        )
+    ]
+    for fetch in fetches:
+        fetch.start()
+
     barrier = pltpu.get_barrier_semaphore()
     for other in (*targets, partner):
         pl.semaphore_signal(
@@ -125,36 +134,46 @@
 
     window_of = lax.broadcasted_iota(jnp.int32, (windows, length), 1) // bins
     spread = window_of == lax.broadcasted_iota(jnp.int32, (windows, length), 0)
+    bin_of = lax.broadcasted_iota(jnp.int32, (half, LANES), 1) % bins
+    count = 1 + jnp.minimum(bin_of, reach) + jnp.minimum(bins - 1 - bin_of, reach)
+    weight = 1.0 / count.astype(jnp.float32)
+    fetches[0].wait()
     live = lax.dot_general(
         gaps[...].astype(jnp.float32).astype(jnp.bfloat16),
         spread.astype(jnp.float32).astype(jnp.bfloat16),
         (((0,), (0,)), ((), ())),
         preferred_element_type=jnp.float32,
     )
-    bin_of = lax.broadcasted_iota(jnp.int32, (members, LANES), 1) % bins
-    count = 1 + jnp.minimum(bin_of, reach) + jnp.minimum(bins - 1 - bin_of, reach)
-    weight = 1.0 / count.astype(jnp.float32)
-    for at in range(0, length, LANES):
-        cut = slice(at, at + LANES)
-        real = spectra[0, :, cut].astype(jnp.float32)
-        imag = spectra[1, :, cut].astype(jnp.float32)
-        amplitude = jnp.sqrt(real * real + imag * imag)
-        total = amplitude
-        for off in range(1, reach + 1):
-            total += jnp.where(bin_of >= off, pltpu.roll(amplitude, off, 1), 0.0)
-            total += jnp.where(bin_of < bins - off, pltpu.roll(amplitude, LANES - off, 1), 0.0)
-        level = jnp.maximum(total * weight, level_floor)
-        factor = live[:, cut] / level
-        blocks[me, :, at : at + LANES] = (real * factor).astype(jnp.bfloat16)
-        blocks[me, :, length + at : length + at + LANES] = (imag * factor).astype(jnp.bfloat16)
-
+    fetches[1].wait()
+
+    def whiten(h):
+        rows = slice(h * half, (h + 1) * half)
+        for at in range(0, length, LANES):
+            cut = slice(at, at + LANES)
+            real = spectra[0, rows, cut].astype(jnp.float32)
+            imag = spectra[1, rows, cut].astype(jnp.float32)
+            amplitude = jnp.sqrt(real * real + imag * imag)
+            total = amplitude
+            for off in range(1, reach + 1):
+                total += jnp.where(bin_of >= off, pltpu.roll(amplitude, off, 1), 0.0)
+                total += jnp.where(bin_of < bins - off, pltpu.roll(amplitude, LANES - off, 1), 0.0)
+            level = jnp.maximum(total * weight, level_floor)
+            factor = live[rows, cut] / level
+            blocks[me, rows, at : at + LANES] = (real * factor).astype(jnp.bfloat16)
+            blocks[me, rows, length + at : length + at + LANES] = (imag * factor).astype(
+                jnp.bfloat16
+            )
+
+    whiten(0)
     pl.semaphore_wait(barrier, 3)
-
-    for h in (0, 1):
-        ring(0, 0, h).start()
-        ring(1, 0, 1 - h).start()
+    ring(0, 0, 0).start()
+    whiten(1)
+    ring(1, 0, 1).start()
+    ring(0, 0, 1).start()
+    ring(1, 0, 0).start()
     for h in (0, 1):
         pair(0, 0, h).start()
+    fetches[2].wait()
 
     def modulate(lag, carry):
         cosine = tables[0, pl.ds(lag, 1), :]
@@ -248,9 +267,13 @@
             pltpu.VMEM((devices, members, 2 * length), jnp.bfloat16),
             pltpu.VMEM((LAGS * members, 2 * length), jnp.bfloat16),
         ],
-        in_specs=[vmem] * 3,
+        in_specs=[pl.BlockSpec(memory_space=pltpu.HBM)] * 3,
         out_specs=[vmem] * 3,
         scratch_shapes=[
+            pltpu.VMEM(spectra.shape, spectra.dtype),
+            pltpu.VMEM(gap_mask.shape[::-1], gap_mask.dtype),
+            pltpu.VMEM(tables.shape, jnp.float32),
+            pltpu.SemaphoreType.DMA((3,)),
             pltpu.SemaphoreType.DMA((2, far, 2)),
             pltpu.SemaphoreType.DMA((2, far, 2)),
             pltpu.SemaphoreType.DMA((2, far + 1, 2)),

time: 27.1 us -> 27.4 us (1.011)
  Pallas kernels: 24.5 us -> 24.8 us
    pallas_call x1, Pallas kernels: 23 us -> 23.4 us  [per_device(): pl.pallas_call(functools.partial(kernel, devices), out_shape=[pltpu.VMEM(...]
where the time goes in v3:
time: 27.4 us; the launch traced here: 27.2 us
  Pallas kernels  24.8 us (91%)
  local copies, waits for them, and re-layouts  2.36 us (9%)
    pallas_call x1, Pallas kernels, per_device(): pl.pallas_call(functools.partial(kernel, devices), out_shape=[pltpu.VMEM(...  23.4 us
    unnamed x6, local copies, waits for them, and re-layouts  2.36 us
    pallas_call x1, Pallas kernels, per_device(): pl.pallas_call(functools.partial(finish, devices), out_shape=jax.ShapeDty...  1.44 us

profile of v3, /device:TPU:0, one launch (start us, length us, event | category | flops | bytes accessed | tf_op | source)
XLA Modules:
  0.0 27.2 jit_solution(18284662443615641039)
XLA Ops:
  0.0 0.0 copy-start
  0.0 0.9 %copy-done = bf16[2,64,768]{2,1,0:T(8,128)(2,1)S(1)} copy-done((bf16[2,64,768]{2,1,0:T(8,128)(2,1)S(1)}, bf16[2,64,768]{2,1,0:T(8,128)(2,1)}, u32[]{:S(2)}) %copy-start) | copy-done | bytes 196632
  0.9 0.0 copy-start.1
  0.9 0.7 %copy-done.1 = s32[64,48]{0,1:T(8,128)S(1)} copy-done((s32[64,48]{0,1:T(8,128)S(1)}, s32[64,48]{0,1:T(8,128)}, u32[]{:S(2)}) %copy-start.1) | copy-done | bytes 12312
  1.7 0.0 copy-start.2
  1.7 0.7 %copy-done.2 = f32[2,8,128]{2,1,0:T(8,128)S(1)} copy-done((f32[2,8,128]{2,1,0:T(8,128)S(1)}, f32[2,8,128]{2,1,0:T(8,128)}, u32[]{:S(2)}) %copy-start.2) | copy-done | bytes 8216
  2.4 23.4 %shard_map.37 = (f32[8,64,1024]{2,1,0:T(8,128)S(1)}, bf16[16,64,1536]{2,1,0:T(8,128)(2,1)S(1)}, bf16[512,1536]{1,0:T(8,128)(2,1)S(1)}) custom-call(bf16[2,64,768]{2,1,0:T(8,128)(2,1)S(1)} %copy-done, s32[48,64]{1,0:T(8,128)S(1)} %bitcast.1, f32[2,8,128]{2,1,0:T(8,128)S(1)} %copy-done.2), custom_call_target="tpu_custom_call" | custom-call | tf_op jit(solution)/shard_map/pallas_call | solution.py:263
  25.7 1.4 %shard_map.38 = f32[8,64,1024]{2,1,0:T(8,128)} custom-call(f32[8,64,1024]{2,1,0:T(8,128)S(1)} %get-tuple-element.8.partial, bf16[16,64,1536]{2,1,0:T(8,128)(2,1)S(1)} %get-tuple-element.9.blocks, bf16[512,1536]{1,0:T(8,128)(2,1)S(1)} %get-tuple-element.10.modulated), custom_call_target="tpu_custom_call" | custom-call | tf_op jit(solution)/shard_map/pallas_call | solution.py:286
Async XLA Ops:
  0.0 0.9 %copy-start = (bf16[2,64,768]{2,1,0:T(8,128)(2,1)S(1)}, bf16[2,64,768]{2,1,0:T(8,128)(2,1)}, u32[]{:S(2)}) copy-start(bf16[2,64,768]{2,1,0:T(8,128)(2,1)} %spectra_in.1) | copy-start | bytes 589828
  0.9 0.7 %copy-start.1 = (s32[64,48]{0,1:T(8,128)S(1)}, s32[64,48]{0,1:T(8,128)}, u32[]{:S(2)}) copy-start(s32[64,48]{0,1:T(8,128)} %param.4) | copy-start | bytes 36868
  1.7 0.7 %copy-start.2 = (f32[2,8,128]{2,1,0:T(8,128)S(1)}, f32[2,8,128]{2,1,0:T(8,128)}, u32[]{:S(2)}) copy-start(f32[2,8,128]{2,1,0:T(8,128)} %constant.2.clone.tables_in) | copy-start | bytes 24580

commit v4 on v3

--- a/solution.py
+++ b/solution.py
@@ -11,6 +11,7 @@
 
 LAGS = 8
 LANES = 128
+VMEM_BYTES = 67043328
 level_floor = 0.3
 first_bin = 96.0
 reach = 2
@@ -259,6 +260,7 @@
     far = devices // 4
     tables = phase_tables(length // gap_mask.shape[1], LAGS, 1.0 / math.sqrt(length))
     result = (LAGS, members, devices * members)
+    kept = 4 * math.prod(result) + 4 * (devices + LAGS) * members * length
     vmem = pl.BlockSpec(memory_space=pltpu.VMEM)
     partial, blocks, modulated = pl.pallas_call(
         functools.partial(kernel, devices),
@@ -280,7 +282,7 @@
             pltpu.SemaphoreType.DMA((2, far + 1, 2)),
         ],
         compiler_params=pltpu.CompilerParams(
-            collective_id=0, has_side_effects=True, vmem_limit_bytes=16 * 1024 * 1024
+            collective_id=0, has_side_effects=True, vmem_limit_bytes=VMEM_BYTES - kept
         ),
     )(spectra, gap_mask.T, jnp.asarray(tables))
     return pl.pallas_call(

time: 27.4 us -> 24.9 us (0.909)
  local copies, waits for them, and re-layouts: 2.36 us -> 0 us
    unnamed x6 -> x0, local copies, waits for them, and re-layouts: 2.36 us -> none
where the time goes in v4:
time: 24.9 us; the launch traced here: 24.8 us
  Pallas kernels  24.8 us (100%)
    pallas_call x1, Pallas kernels, per_device(): pl.pallas_call(functools.partial(kernel, devices), out_shape=[pltpu.VMEM(...  23.3 us
    pallas_call x1, Pallas kernels, per_device(): pl.pallas_call(functools.partial(finish, devices), out_shape=jax.ShapeDty...  1.44 us

profile of v4, /device:TPU:0, one launch (start us, length us, event | category | flops | bytes accessed | tf_op | source)
XLA Modules:
  0.0 24.8 jit_solution(6548641222777181282)
XLA Ops:
  0.0 23.3 %shard_map.37 = (f32[8,64,1024]{2,1,0:T(8,128)S(1)}, bf16[16,64,1536]{2,1,0:T(8,128)(2,1)S(1)}, bf16[512,1536]{1,0:T(8,128)(2,1)S(1)}) custom-call(bf16[2,64,768]{2,1,0:T(8,128)(2,1)} %spectra_in.1, s32[48,64]{1,0:T(8,128)} %bitcast.1, f32[2,8,128]{2,1,0:T(8,128)} %constant.2.clone.tables_in), custom_call_target="tpu_custom_call" | custom-call | tf_op jit(solution)/shard_map/pallas_call | solution.py:265
  23.4 1.4 %shard_map.38 = f32[8,64,1024]{2,1,0:T(8,128)} custom-call(f32[8,64,1024]{2,1,0:T(8,128)S(1)} %get-tuple-element.8.partial, bf16[16,64,1536]{2,1,0:T(8,128)(2,1)S(1)} %get-tuple-element.9.blocks, bf16[512,1536]{1,0:T(8,128)(2,1)S(1)} %get-tuple-element.10.modulated), custom_call_target="tpu_custom_call" | custom-call | tf_op jit(solution)/shard_map/pallas_call | solution.py:288

commit v5 on v4

--- a/solution.py
+++ b/solution.py
@@ -11,6 +11,7 @@
 
 LAGS = 8
 LANES = 128
+PIECES = 4
 VMEM_BYTES = 67043328
 level_floor = 0.3
 first_bin = 96.0
@@ -81,7 +82,8 @@
     windows = gaps.shape[0]
     bins = length // windows
     lag_count = out.shape[0]
-    half = members // 2
+    height = members // PIECES
+    order = [[(i + way * PIECES // 2) % PIECES for i in range(PIECES)] for way in (0, 1)]
     chips = devices // 2
     far = chips // 2
 
@@ -99,7 +101,7 @@
         return chip_at(spot - distance if way == 0 else spot + distance)
 
     def piece(block, h):
-        return blocks.at[block, pl.ds(h * half, half), :]
+        return blocks.at[block, pl.ds(h * height, height), :]
 
     def ring(way, step, h, incoming=False):
         place = piece(source_chip(way, step + 1 if incoming else step) * 2 + core, h)
@@ -135,7 +137,7 @@
 
     window_of = lax.broadcasted_iota(jnp.int32, (windows, length), 1) // bins
     spread = window_of == lax.broadcasted_iota(jnp.int32, (windows, length), 0)
-    bin_of = lax.broadcasted_iota(jnp.int32, (half, LANES), 1) % bins
+    bin_of = lax.broadcasted_iota(jnp.int32, (height, LANES), 1) % bins
     count = 1 + jnp.minimum(bin_of, reach) + jnp.minimum(bins - 1 - bin_of, reach)
     weight = 1.0 / count.astype(jnp.float32)
     fetches[0].wait()
@@ -148,7 +150,7 @@
     fetches[1].wait()
 
     def whiten(h):
-        rows = slice(h * half, (h + 1) * half)
+        rows = slice(h * height, (h + 1) * height)
         for at in range(0, length, LANES):
             cut = slice(at, at + LANES)
             real = spectra[0, rows, cut].astype(jnp.float32)
@@ -165,14 +167,16 @@
                 jnp.bfloat16
             )
 
-    whiten(0)
-    pl.semaphore_wait(barrier, 3)
-    ring(0, 0, 0).start()
-    whiten(1)
-    ring(1, 0, 1).start()
-    ring(0, 0, 1).start()
-    ring(1, 0, 0).start()
-    for h in (0, 1):
+    for i in range(PIECES // 2):
+        for way in (0, 1):
+            whiten(order[way][i])
+            if i == 0 and way == 0:
+                pl.semaphore_wait(barrier, 3)
+            ring(way, 0, order[way][i]).start()
+    for i in range(PIECES // 2, PIECES):
+        for way in (0, 1):
+            ring(way, 0, order[way][i]).start()
+    for h in range(PIECES):
         pair(0, 0, h).start()
     fetches[2].wait()
 
@@ -198,59 +202,60 @@
         out[:, :, columns] = tile_product(modulated, blocks, tile, lag_count)
 
     def pair_ready(way, distance):
-        for h in (0, 1):
+        for h in range(PIECES):
             pair(way, distance, h, incoming=True).wait_recv()
 
-    def take(step, h, last):
-        for way in (0, 1):
-            part = h if way == 0 else 1 - h
-            ring(way, step - 1, part, incoming=True).wait_recv()
-            if not last or h == 0:
-                ring(way, step, part).start()
-            pair(way, step, part).start()
-
-    take(1, 0, far == 2)
-    pair_ready(0, 0)
-    correlate(0, 0)
-    take(1, 1, far == 2)
-
-    def onward(step, last):
-        take(step, 0, last)
-        pair_ready(0, step - 1)
-        correlate(0, step - 1)
-        take(step, 1, last)
-        pair_ready(1, step - 1)
-        correlate(1, step - 1)
+    def take(step, i, last):
+        for way in (0, 1):
+            h = order[way][i]
+            ring(way, step - 1, h, incoming=True).wait_recv()
+            if not last or i < PIECES // 2:
+                ring(way, step, h).start()
+            pair(way, step, h).start()
+
+    def onward(step, last, tiles):
+        for i in range(PIECES):
+            take(step, i, last)
+            if 1 <= i <= len(tiles):
+                way = tiles[i - 1]
+                pair_ready(way, step - 1)
+                correlate(way, step - 1)
+
+    onward(1, far == 2, (0,))
 
     def body(step, carry):
-        onward(step, False)
+        onward(step, False, (0, 1))
         return carry
 
     lax.fori_loop(2, far - 1, body, 0)
-    onward(far - 1, True)
+    onward(far - 1, True, (0, 1))
 
     pair_ready(0, far - 1)
     correlate(0, far - 1)
+    for i in range(PIECES // 2):
+        for way in (0, 1):
+            h = order[way][i]
+            ring(way, far - 1, h, incoming=True).wait_recv()
+            pair(way, far, h).start()
     pair_ready(1, far - 1)
-    for way in (0, 1):
-        ring(way, far - 1, way, incoming=True).wait_recv()
-        pair(way, far, way).start()
     correlate(1, far - 1)
     for way in (0, 1):
-        pair(way, far, way, incoming=True).wait_recv()
+        for h in order[way][: PIECES // 2]:
+            pair(way, far, h, incoming=True).wait_recv()
 
     def drain(step, carry):
         for way in (0, 1):
-            for h in (0, 1):
+            for h in range(PIECES):
                 ring(way, step, h).wait_send()
                 pair(way, step + 1, h).wait_send()
         return carry
 
     lax.fori_loop(0, far - 1, drain, 0)
     for way in (0, 1):
-        ring(way, far - 1, way).wait_send()
-        pair(way, far, way).wait_send()
-    for h in (0, 1):
+        for h in order[way][: PIECES // 2]:
+            ring(way, far - 1, h).wait_send()
+            pair(way, far, h).wait_send()
+    for h in range(PIECES):
         pair(0, 0, h).wait_send()
 
 
@@ -276,10 +281,10 @@
             pltpu.VMEM(gap_mask.shape[::-1], gap_mask.dtype),
             pltpu.VMEM(tables.shape, jnp.float32),
             pltpu.SemaphoreType.DMA((3,)),
-            pltpu.SemaphoreType.DMA((2, far, 2)),
-            pltpu.SemaphoreType.DMA((2, far, 2)),
-            pltpu.SemaphoreType.DMA((2, far + 1, 2)),
-            pltpu.SemaphoreType.DMA((2, far + 1, 2)),
+            pltpu.SemaphoreType.DMA((2, far, PIECES)),
+            pltpu.SemaphoreType.DMA((2, far, PIECES)),
+            pltpu.SemaphoreType.DMA((2, far + 1, PIECES)),
+            pltpu.SemaphoreType.DMA((2, far + 1, PIECES)),
         ],
         compiler_params=pltpu.CompilerParams(
             collective_id=0, has_side_effects=True, vmem_limit_bytes=VMEM_BYTES - kept

time: 24.9 us -> 25 us (level)
  no operation moved by 1% of the time
where the time goes in v5:
time: 25 us; the launch traced here: 24.8 us
  Pallas kernels  24.8 us (99%)
    pallas_call x1, Pallas kernels, per_device(): pl.pallas_call(functools.partial(kernel, devices), out_shape=[pltpu.VMEM(...  23.4 us
    pallas_call x1, Pallas kernels, per_device(): pl.pallas_call(functools.partial(finish, devices), out_shape=jax.ShapeDty...  1.45 us

profile of v5, /device:TPU:0, one launch (start us, length us, event | category | flops | bytes accessed | tf_op | source)
XLA Modules:
  0.0 24.8 jit_solution(4002081826758365479)
XLA Ops:
  0.0 23.4 %shard_map.37 = (f32[8,64,1024]{2,1,0:T(8,128)S(1)}, bf16[16,64,1536]{2,1,0:T(8,128)(2,1)S(1)}, bf16[512,1536]{1,0:T(8,128)(2,1)S(1)}) custom-call(bf16[2,64,768]{2,1,0:T(8,128)(2,1)} %spectra_in.1, s32[48,64]{1,0:T(8,128)} %bitcast.1, f32[2,8,128]{2,1,0:T(8,128)} %constant.2.clone.tables_in), custom_call_target="tpu_custom_call" | custom-call | tf_op jit(solution)/shard_map/pallas_call | solution.py:270
  23.4 1.4 %shard_map.38 = f32[8,64,1024]{2,1,0:T(8,128)} custom-call(f32[8,64,1024]{2,1,0:T(8,128)S(1)} %get-tuple-element.8.partial, bf16[16,64,1536]{2,1,0:T(8,128)(2,1)S(1)} %get-tuple-element.9.blocks, bf16[512,1536]{1,0:T(8,128)(2,1)S(1)} %get-tuple-element.10.modulated), custom_call_target="tpu_custom_call" | custom-call | tf_op jit(solution)/shard_map/pallas_call | solution.py:293

commit v6 on v5

--- a/solution.py
+++ b/solution.py
@@ -12,6 +12,7 @@
 LAGS = 8
 LANES = 128
 PIECES = 4
+GROUPS = 4
 VMEM_BYTES = 67043328
 level_floor = 0.3
 first_bin = 96.0
@@ -67,11 +68,21 @@
         return carry
 
     lax.fori_loop(1, chips, begin, 0)
-    last[...] = tile_product(modulated, blocks, far_tile, lag_count)
-    tail = pltpu.make_async_copy(last, out.at[:, :, columns(far_tile)], done.at[0])
-    tail.start()
+    each = lag_count // GROUPS
+    tails = []
+    for group in range(GROUPS):
+        lags = slice(group * each, (group + 1) * each)
+        rows = modulated.at[group * each * members : (group + 1) * each * members]
+        last[lags] = tile_product(rows, blocks, far_tile, each)
+        tails.append(
+            pltpu.make_async_copy(
+                last.at[lags], out.at[lags, :, columns(far_tile)], done.at[chips + group]
+            )
+        )
+        tails[-1].start()
     lax.fori_loop(1, chips, end, 0)
-    tail.wait()
+    for tail in tails:
+        tail.wait()
 
 
 def kernel(
@@ -297,7 +308,7 @@
         out_specs=pl.BlockSpec(memory_space=pl.ANY),
         scratch_shapes=[
             pltpu.VMEM((LAGS, members, 2 * members), jnp.float32),
-            pltpu.SemaphoreType.DMA((devices // 2,)),
+            pltpu.SemaphoreType.DMA((devices // 2 + GROUPS,)),
         ],
         compiler_params=pltpu.CompilerParams(vmem_limit_bytes=16 * 1024 * 1024),
     )(partial, blocks, modulated)

time: 25 us -> 25 us (level)
  no operation moved by 1% of the time
where the time goes in v6:
time: 25 us; the launch traced here: 24.8 us
  Pallas kernels  24.8 us (99%)
    pallas_call x1, Pallas kernels, per_device(): pl.pallas_call(functools.partial(kernel, devices), out_shape=[pltpu.VMEM(...  23.4 us
    pallas_call x1, Pallas kernels, per_device(): pl.pallas_call(functools.partial(finish, devices), out_shape=jax.ShapeDty...  1.44 us

profile of v6, /device:TPU:0, one launch (start us, length us, event | category | flops | bytes accessed | tf_op | source)
XLA Modules:
  0.0 24.8 jit_solution(18357260278228363047)
XLA Ops:
  0.0 23.4 %shard_map.37 = (f32[8,64,1024]{2,1,0:T(8,128)S(1)}, bf16[16,64,1536]{2,1,0:T(8,128)(2,1)S(1)}, bf16[512,1536]{1,0:T(8,128)(2,1)S(1)}) custom-call(bf16[2,64,768]{2,1,0:T(8,128)(2,1)} %spectra_in.1, s32[48,64]{1,0:T(8,128)} %bitcast.1, f32[2,8,128]{2,1,0:T(8,128)} %constant.2.clone.tables_in), custom_call_target="tpu_custom_call" | custom-call | tf_op jit(solution)/shard_map/pallas_call | solution.py:281
  23.4 1.4 %shard_map.38 = f32[8,64,1024]{2,1,0:T(8,128)} custom-call(f32[8,64,1024]{2,1,0:T(8,128)S(1)} %get-tuple-element.8.partial, bf16[16,64,1536]{2,1,0:T(8,128)(2,1)S(1)} %get-tuple-element.9.blocks, bf16[512,1536]{1,0:T(8,128)(2,1)S(1)} %get-tuple-element.10.modulated), custom_call_target="tpu_custom_call" | custom-call | tf_op jit(solution)/shard_map/pallas_call | solution.py:304

commit v7 on v5

--- a/solution.py
+++ b/solution.py
@@ -44,34 +44,15 @@
     return sums.reshape(lag_count, members, 2 * members)
 
 
-def finish(devices, partial, blocks, modulated, out, last, done):
-    chips = devices // 2
-    lag_count, members = partial.shape[0], partial.shape[1]
-    width = 2 * members
-    spot = ring_spot(chips, lax.axis_index("blk") // 2)
-    far_tile = ring_chip(chips, spot + chips // 2)
-
-    def columns(tile):
-        return pl.ds(pl.multiple_of(tile * width, width), width)
-
-    def place(away):
-        cut = columns(ring_chip(chips, spot + chips // 2 + away))
-        return pltpu.make_async_copy(partial.at[:, :, cut], out.at[:, :, cut], done.at[away])
-
-    def begin(away, carry):
-        place(away).start()
-        return carry
-
-    def end(away, carry):
-        place(away).wait()
-        return carry
-
-    lax.fori_loop(1, chips, begin, 0)
-    last[...] = tile_product(modulated, blocks, far_tile, lag_count)
-    tail = pltpu.make_async_copy(last, out.at[:, :, columns(far_tile)], done.at[0])
-    tail.start()
-    lax.fori_loop(1, chips, end, 0)
-    tail.wait()
+def finish(whole, out, done):
+    copies = [
+        pltpu.make_async_copy(whole.at[lag], out.at[lag], done.at[lag])
+        for lag in range(whole.shape[0])
+    ]
+    for copy in copies:
+        copy.start()
+    for copy in copies:
+        copy.wait()
 
 
 def kernel(
@@ -242,6 +223,7 @@
     for way in (0, 1):
         for h in order[way][: PIECES // 2]:
             pair(way, far, h, incoming=True).wait_recv()
+    correlate(0, far)
 
     def drain(step, carry):
         for way in (0, 1):
@@ -267,7 +249,7 @@
     result = (LAGS, members, devices * members)
     kept = 4 * math.prod(result) + 4 * (devices + LAGS) * members * length
     vmem = pl.BlockSpec(memory_space=pltpu.VMEM)
-    partial, blocks, modulated = pl.pallas_call(
+    whole, _, _ = pl.pallas_call(
         functools.partial(kernel, devices),
         out_shape=[
             pltpu.VMEM(result, jnp.float32),
@@ -291,16 +273,13 @@
         ),
     )(spectra, gap_mask.T, jnp.asarray(tables))
     return pl.pallas_call(
-        functools.partial(finish, devices),
+        finish,
         out_shape=jax.ShapeDtypeStruct(result, jnp.float32),
-        in_specs=[vmem] * 3,
+        in_specs=[vmem],
         out_specs=pl.BlockSpec(memory_space=pl.ANY),
-        scratch_shapes=[
-            pltpu.VMEM((LAGS, members, 2 * members), jnp.float32),
-            pltpu.SemaphoreType.DMA((devices // 2,)),
-        ],
+        scratch_shapes=[pltpu.SemaphoreType.DMA((LAGS,))],
         compiler_params=pltpu.CompilerParams(vmem_limit_bytes=16 * 1024 * 1024),
-    )(partial, blocks, modulated)
+    )(whole)
 
 
 def solution(mesh):

time: 25 us -> 28 us (1.12)
  Pallas kernels: 24.8 us -> 27.8 us
    pallas_call x1, Pallas kernels: 23.4 us -> 26.5 us  [per_device(): pl.pallas_call(functools.partial(kernel, devices), out_shape=[pltpu.VMEM(...]
where the time goes in v7:
time: 28 us; the launch traced here: 27.9 us
  Pallas kernels  27.8 us (99%)
    pallas_call x1, Pallas kernels, per_device(): pl.pallas_call(functools.partial(kernel, devices), out_shape=[pltpu.VMEM(...  26.5 us
    pallas_call x1, Pallas kernels, per_device(): pl.pallas_call(finish, out_shape=jax.ShapeDtypeStruct(result, jnp.float32...  1.38 us

profile of v7, /device:TPU:0, one launch (start us, length us, event | category | flops | bytes accessed | tf_op | source)
XLA Modules:
  0.0 27.9 jit_solution(3629794196650497062)
XLA Ops:
  0.0 26.5 %shard_map.37 = (f32[8,64,1024]{2,1,0:T(8,128)S(1)}, bf16[16,64,1536]{2,1,0:T(8,128)(2,1)}, bf16[512,1536]{1,0:T(8,128)(2,1)}) custom-call(bf16[2,64,768]{2,1,0:T(8,128)(2,1)} %spectra_in.1, s32[48,64]{1,0:T(8,128)} %bitcast.1, f32[2,8,128]{2,1,0:T(8,128)} %constant.2.clone.tables_in), custom_call_target="tpu_custom_call" | custom-call | tf_op jit(solution)/shard_map/pallas_call | solution.py:252
  26.5 1.4 %shard_map.38 = f32[8,64,1024]{2,1,0:T(8,128)} custom-call(f32[8,64,1024]{2,1,0:T(8,128)S(1)} %get-tuple-element.6.whole), custom_call_target="tpu_custom_call" | custom-call | tf_op jit(solution)/shard_map/pallas_call | solution.py:275
